TPU v7x, 32 devices: a whole 2x2x4 slice. The times are simulated.
32 devices in a mesh: region: 8 (over z, core), member: 4 (over y, x).
Axes of the slice: x: 2, y: 2, z: 4, core: 2. Of those that a mesh axis runs over, the one named last changes fastest.
Arguments:
- positions: float32 [3, 12288], P(None, ('region', 'member'))
- forces: float32 [3, 12288], P(None, ('region', 'member')), may hold values from -6 to 6
- blob_platelet: int32 [12288], P(('region', 'member')), may hold values from 0 to 8, as said below
- blob_rank: int32 [12288], P(('region', 'member')), may hold values from 0 to 161, as said below
- platelet_owner: int32 [64], P('region'), may hold values from 0 to 7, as said below
- pair_list: int32 [96, 8], P(('region', 'member')), may hold values from 0 to 23, as said below
- pair_count: int32 [96], P(('region', 'member')), may hold values from 1 to 8, as said below
- preconditioner: bfloat16 [64, 486, 486], P(('region', 'member')), may hold values from -0.25 to 0.25
Outputs:
- blob_velocity: float32 [3, 12288], P(None, ('region', 'member'))
- body_velocity: float32 [64, 486], P(('region', 'member'))
Inputs may be any that keep to these rules, and one draw needn't show every extreme that they name: `blob_platelet`: in each slab every platelet id below 8 appears on exactly 162 slots, and 8 marks an empty slot. Every device holds exactly 324 live blobs, of which at most 121 belong to platelets whose owner slots lie on one member; that bound is met in every slab. `blob_rank`: the 162 blobs of one platelet have distinct ranks; empty slots have rank 0. `platelet_owner`: the 8 entries of one slab are a permutation; owner slot o lies on member o // 2 of that slab. `pair_list`: the entries of one target tile are distinct, and entry 0 is the tile itself, 6 plus its index within its slab. `pair_count`: some tile has 8 in every draw.
All inputs are finite; a program needn't handle non-finite values.
Results may differ from a plain program's by a relative error of at most 0.0029.
Values sent between devices are 32-bit elements; how exact they have to be, the bound alone decides.
A program may use at most 64 MiB of HBM per device.

v0:
```python
import math
import jax
import jax.numpy as jnp
from jax import lax
from jax.sharding import PartitionSpec as P

TILE = 128
PB = 162
PLAT_DEV = 2
soft_square = 1.0


def padded(cells, sides, width):
    for axis, dim in sides:
        count = lax.axis_size(axis)
        ends = count - 1
        head = lax.slice_in_dim(cells, 0, width, axis=dim)
        tail = lax.slice_in_dim(cells, cells.shape[dim] - width, cells.shape[dim], axis=dim)
        cells = jnp.concatenate(
            [
                lax.ppermute(tail, axis, [(i, (i + 1) % count) for i in range(ends)]),
                cells,
                lax.ppermute(head, axis, [((i + 1) % count, i) for i in range(ends)]),
            ],
            axis=dim,
        )
    return cells


def stokes_sum(targets, sources, pushes):
    force = pushes[:, :, None, :]
    separation = targets[:, :, :, None] - sources[:, :, None, :]
    dist_square = jnp.sum(separation * separation, axis=0)
    force_along = jnp.sum(separation * force, axis=0)
    kernel_weight = 1.0 / (
        8.0 * math.pi * (dist_square + soft_square) * jnp.sqrt(dist_square + soft_square)
    )
    direct = ((dist_square + 2.0 * soft_square) * force + separation * force_along) * kernel_weight
    flip_source = jnp.array([1.0, 1.0, -1.0], jnp.float32)[:, None, None]
    flip_pair = jnp.array([1.0, 1.0, -1.0], jnp.float32)[:, None, None, None]
    unit_normal = jnp.array([0.0, 0.0, 1.0], jnp.float32)[:, None, None, None]
    height = sources[2][:, None, :]
    image_gap = targets[:, :, :, None] - (sources * flip_source)[:, :, None, :]
    image_square = jnp.sum(image_gap * image_gap, axis=0)
    inverse_one = 1.0 / jnp.sqrt(image_square)
    inverse_three = inverse_one * inverse_one * inverse_one
    inverse_five = inverse_three * inverse_one * inverse_one
    image_along = jnp.sum(image_gap * force, axis=0)
    mirrored = force * flip_pair
    mirror_along = jnp.sum(image_gap * mirrored, axis=0)
    normal_gap = image_gap[2]
    stokes_image = force * inverse_one + image_gap * image_along * inverse_three
    doublet = height * (mirrored * inverse_three - 3.0 * image_gap * mirror_along * inverse_five)
    doublet = doublet + unit_normal * mirror_along * inverse_three
    doublet = doublet - (mirrored * normal_gap + image_gap * mirrored[2]) * inverse_three
    doublet = doublet + 3.0 * image_gap * normal_gap * mirror_along * inverse_five
    wall_term = (2.0 * height * doublet - stokes_image) * (1.0 / (8.0 * math.pi))
    return jnp.sum(direct + wall_term, axis=3)


def on_device(
    positions,
    forces,
    blob_platelet,
    blob_rank,
    platelet_owner,
    pair_list,
    pair_count,
    preconditioner,
):
    blob_count = positions.shape[1]
    plate_count = platelet_owner.shape[0]
    is_live = blob_platelet < plate_count
    live_mask = is_live.astype(jnp.float32)
    own_blobs = jnp.concatenate([positions, forces * live_mask[None, :]], 0)
    region_all = lax.all_gather(own_blobs, "member", axis=1, tiled=True)
    extended = padded(region_all, (("region", 1),), region_all.shape[1] // 2)
    ext_blocks = extended.reshape(6, extended.shape[1] // TILE, TILE)
    targets = positions.reshape(3, blob_count // TILE, TILE)
    pair_rounds = jnp.max(pair_count)

    def one_slot(pair_slot, accumulated):
        source_ids = lax.dynamic_index_in_dim(pair_list, pair_slot, 1, keepdims=False)
        picked = jnp.take(ext_blocks, source_ids, axis=1)
        keep_mask = (pair_slot < pair_count).astype(jnp.float32)
        return accumulated + keep_mask[None, :, None] * stokes_sum(targets, picked[:3], picked[3:])

    velocity = lax.fori_loop(0, pair_rounds, one_slot, jnp.zeros(targets.shape, jnp.float32))
    blob_velocity = velocity.reshape(3, blob_count)
    plate_match = blob_platelet[:, None] == jnp.arange(plate_count, dtype=jnp.int32)[None, :]
    slot_of = jnp.sum(jnp.where(plate_match, platelet_owner[None, :], 0), axis=1)
    whole_body = PLAT_DEV * PB
    region_target = jnp.where(is_live, slot_of * PB + blob_rank, plate_count * PB)
    all_velocity, all_target = (
        lax.all_gather(blob_velocity, "member", axis=1, tiled=True),
        lax.all_gather(region_target, "member", axis=0, tiled=True),
    )
    local_index = all_target - lax.axis_index("member") * whole_body
    local_index = jnp.where(
        (local_index >= 0) & (local_index < whole_body), local_index, whole_body
    )
    body_flat = (
        jnp.zeros((3, whole_body), jnp.float32).at[:, local_index].set(all_velocity, mode="drop")
    )
    body_in = (
        body_flat.reshape(3, PLAT_DEV, PB)
        .transpose(1, 0, 2)
        .reshape(PLAT_DEV, 3 * PB)
        .astype(jnp.bfloat16)
    )
    body_velocity = jnp.einsum(
        "pab,pb->pa", preconditioner, body_in, preferred_element_type=jnp.float32
    )
    return (blob_velocity, body_velocity)


def solution(mesh):
    placed = (
        P(None, ("region", "member")),
        P(None, ("region", "member")),
        P(("region", "member")),
        P(("region", "member")),
        P("region"),
        P(("region", "member"), None),
        P(("region", "member")),
        P(("region", "member"), None, None),
    )
    return jax.shard_map(
        on_device,
        mesh=mesh,
        in_specs=placed,
        out_specs=(P(None, ("region", "member")), P(("region", "member"), None)),
        check_vma=False,
    )
```

profile of v0, /device:TPU:0, one launch (start us, length us, event | category | flops | bytes accessed | tf_op | source)
XLA Modules:
  0.0 66.3 jit_solution(10608921622263139967)
XLA Ops:
  0.7 0.9 %select_reduce_fusion = s32[384]{0:T(512)S(1)} fusion(s32[8]{0:T(128)} %param.17, s32[384]{0:T(512)} %param.15), kind=kLoop, calls=%fused_computation.62 | loop fusion | flops 8832 | bytes 3104 | tf_op jit(solution)/shard_map/reduce_sum | solution.py:91
  1.6 0.7 copy-done.6
  2.2 0.7 %copy-done.1 = f32[3,384]{1,0:T(4,128)S(1)} copy-done((f32[3,384]{1,0:T(4,128)S(1)}, f32[3,384]{1,0:T(4,128)}, u32[]{:S(2)}) %copy-start.1) | copy-done | bytes 4632
  2.9 9.7 %all_gather.9 = f32[6,1536]{1,0:T(8,128)S(1)} all-gather(f32[6,384]{1,0:T(8,128)S(1)} %pad_maximum_fusion), channel_id=1, replica_groups=mesh['region'=8,'member'=4] {'member'}, dimensions={1}, use_global_device_ids=true | all-gather | bytes 46080 | tf_op jit(solution)/shard_map/all_gather | solution.py:76
  12.7 1.3 %collective-permute-start.1 = (f32[6,768]{1,0:T(8,128)S(1)}, f32[6,768]{1,0:T(8,128)S(1)}, u32[]{:S(2)}, u32[]{:S(2)}) collective-permute-start(f32[6,768]{1,0:T(8,128)S(1)} %get-tuple-element.180), channel_id=1, source_target_pairs={{4,0},{8,4},{12,8},{16,12},{20,16},{24,20},{28,24},{5,1},{9,5},{13... | collective-permute-start | bytes 55304 | tf_op jit(solution)/shard_map/ppermute | solution.py:23
  14.0 3.0 %collective-permute-start = (f32[6,768]{1,0:T(8,128)S(1)}, f32[6,768]{1,0:T(8,128)S(1)}, u32[]{:S(2)}, u32[]{:S(2)}) collective-permute-start(f32[6,768]{1,0:T(8,128)S(1)} %get-tuple-element.179), channel_id=1, source_target_pairs={{0,4},{4,8},{8,12},{12,16},{16,20},{20,24},{24,28},{1,5},{5,9},{9,... | collective-permute-start | bytes 55304 | tf_op jit(solution)/shard_map/ppermute | solution.py:21
  17.0 8.1 %all-gather = s32[4,1,384]{2,1,0:T(1,128)S(1)} all-gather(s32[1,1,384]{2,1,0:T(1,128)S(1)} %reshape.93), channel_id=1, replica_groups=mesh['region'=8,'member'=4] {'member'}, dimensions={0}, use_global_device_ids=true | all-gather | bytes 7680 | tf_op jit(solution)/shard_map/all_gather | solution.py:96
  25.2 0.7 copy-done.8
  25.9 0.6 copy-done.9
  26.5 0.6 reduce_max.9
  27.2 0.6 copy-done.3
  27.8 22.2 %while.13 = (s32[]{:T(128)}, f32[3,3,128]{2,1,0:T(4,128)S(1)}, s32[]{:T(128)}, s32[3]{0:T(128)S(1)}, f32[3,384]{1,0:T(4,128)}, /*index=5*/s32[3,8]{0,1:T(8,128)S...) while((s32[]{:T(128)}, f32[3,3,128]{2,1,0:T(4,128)S(1)}, ...), condition=%wide.wide.region_8.9_spmd.clone.clone, body=%wide.wide.region_1.8_spmd.sunk.clone.clone.sunk | while | flops 6790173 | bytes 6481697 | solution.py:88
  28.5 0.6 gather_fusion
  29.2 0.3 fusion.34
  29.7 0.1 broadcast_add_fusion.3
  29.8 1.0 %fusion.35 = f32[3,3,128]{2,1,0:T(4,128)S(1)} fusion(f32[3,128,128]{2,1,0:T(8,128)S(1)} %get-tuple-element.308, f32[3,128,128]{2,1,0:T(8,128)S(1)} %get-tuple-element.311, f32[3,128,128]{2,1,0:T(8,128)S(1)} %get-tuple-element.312, f32[3,128]{1,0:T(4,128)S(1)} %get-tuple-element.313, f32[3,128,128]{2,1,0:T(8,128)S(1)} %slice_bitcast_fusion.3, ...), kind=kLoop, calls=%fused_computation.17.clone.clone.1 | loop fusion | flops 4717440 | bytes 2194956 | tf_op jit(solution)/shard_map/while/body/reduce_sum | solution.py:58
  31.6 0.6 gather_fusion
  32.3 0.3 fusion.34
  32.7 0.1 broadcast_add_fusion.3
  32.9 1.0 %fusion.35 = f32[3,3,128]{2,1,0:T(4,128)S(1)} fusion(f32[3,128,128]{2,1,0:T(8,128)S(1)} %get-tuple-element.308, f32[3,128,128]{2,1,0:T(8,128)S(1)} %get-tuple-element.311, f32[3,128,128]{2,1,0:T(8,128)S(1)} %get-tuple-element.312, f32[3,128]{1,0:T(4,128)S(1)} %get-tuple-element.313, f32[3,128,128]{2,1,0:T(8,128)S(1)} %slice_bitcast_fusion.3, ...), kind=kLoop, calls=%fused_computation.17.clone.clone.1 | loop fusion | flops 4717440 | bytes 2194956 | tf_op jit(solution)/shard_map/while/body/reduce_sum | solution.py:58
  34.7 0.6 gather_fusion
  35.4 0.3 fusion.34
  35.8 0.1 broadcast_add_fusion.3
  35.9 1.0 %fusion.35 = f32[3,3,128]{2,1,0:T(4,128)S(1)} fusion(f32[3,128,128]{2,1,0:T(8,128)S(1)} %get-tuple-element.308, f32[3,128,128]{2,1,0:T(8,128)S(1)} %get-tuple-element.311, f32[3,128,128]{2,1,0:T(8,128)S(1)} %get-tuple-element.312, f32[3,128]{1,0:T(4,128)S(1)} %get-tuple-element.313, f32[3,128,128]{2,1,0:T(8,128)S(1)} %slice_bitcast_fusion.3, ...), kind=kLoop, calls=%fused_computation.17.clone.clone.1 | loop fusion | flops 4717440 | bytes 2194956 | tf_op jit(solution)/shard_map/while/body/reduce_sum | solution.py:58
  37.7 0.6 gather_fusion
  38.5 0.3 fusion.34
  38.9 0.1 broadcast_add_fusion.3
  39.0 1.0 %fusion.35 = f32[3,3,128]{2,1,0:T(4,128)S(1)} fusion(f32[3,128,128]{2,1,0:T(8,128)S(1)} %get-tuple-element.308, f32[3,128,128]{2,1,0:T(8,128)S(1)} %get-tuple-element.311, f32[3,128,128]{2,1,0:T(8,128)S(1)} %get-tuple-element.312, f32[3,128]{1,0:T(4,128)S(1)} %get-tuple-element.313, f32[3,128,128]{2,1,0:T(8,128)S(1)} %slice_bitcast_fusion.3, ...), kind=kLoop, calls=%fused_computation.17.clone.clone.1 | loop fusion | flops 4717440 | bytes 2194956 | tf_op jit(solution)/shard_map/while/body/reduce_sum | solution.py:58
  40.8 0.6 gather_fusion
  41.6 0.3 fusion.34
  42.0 0.1 broadcast_add_fusion.3
  42.1 1.0 %fusion.35 = f32[3,3,128]{2,1,0:T(4,128)S(1)} fusion(f32[3,128,128]{2,1,0:T(8,128)S(1)} %get-tuple-element.308, f32[3,128,128]{2,1,0:T(8,128)S(1)} %get-tuple-element.311, f32[3,128,128]{2,1,0:T(8,128)S(1)} %get-tuple-element.312, f32[3,128]{1,0:T(4,128)S(1)} %get-tuple-element.313, f32[3,128,128]{2,1,0:T(8,128)S(1)} %slice_bitcast_fusion.3, ...), kind=kLoop, calls=%fused_computation.17.clone.clone.1 | loop fusion | flops 4717440 | bytes 2194956 | tf_op jit(solution)/shard_map/while/body/reduce_sum | solution.py:58
  43.9 0.6 gather_fusion
  44.6 0.3 fusion.34
  45.1 0.1 broadcast_add_fusion.3
  45.2 1.0 %fusion.35 = f32[3,3,128]{2,1,0:T(4,128)S(1)} fusion(f32[3,128,128]{2,1,0:T(8,128)S(1)} %get-tuple-element.308, f32[3,128,128]{2,1,0:T(8,128)S(1)} %get-tuple-element.311, f32[3,128,128]{2,1,0:T(8,128)S(1)} %get-tuple-element.312, f32[3,128]{1,0:T(4,128)S(1)} %get-tuple-element.313, f32[3,128,128]{2,1,0:T(8,128)S(1)} %slice_bitcast_fusion.3, ...), kind=kLoop, calls=%fused_computation.17.clone.clone.1 | loop fusion | flops 4717440 | bytes 2194956 | tf_op jit(solution)/shard_map/while/body/reduce_sum | solution.py:58
  47.0 0.6 gather_fusion
  47.7 0.3 fusion.34
  48.2 0.1 broadcast_add_fusion.3
  48.3 1.0 %fusion.35 = f32[3,3,128]{2,1,0:T(4,128)S(1)} fusion(f32[3,128,128]{2,1,0:T(8,128)S(1)} %get-tuple-element.308, f32[3,128,128]{2,1,0:T(8,128)S(1)} %get-tuple-element.311, f32[3,128,128]{2,1,0:T(8,128)S(1)} %get-tuple-element.312, f32[3,128]{1,0:T(4,128)S(1)} %get-tuple-element.313, f32[3,128,128]{2,1,0:T(8,128)S(1)} %slice_bitcast_fusion.3, ...), kind=kLoop, calls=%fused_computation.17.clone.clone.1 | loop fusion | flops 4717440 | bytes 2194956 | tf_op jit(solution)/shard_map/while/body/reduce_sum | solution.py:58
  50.1 10.3 %all_gather.11 = f32[3,1536]{1,0:T(4,128)S(1)} all-gather(f32[3,384]{1,0:T(4,128)S(1)} %bitcast.48), channel_id=1, replica_groups=mesh['region'=8,'member'=4] {'member'}, dimensions={1}, use_global_device_ids=true | all-gather | bytes 23040 | tf_op jit(solution)/shard_map/all_gather | solution.py:95
  60.4 0.3 copy.44
  60.7 4.4 %scatter_custom_fusion = f32[3,324]{0,1:T(8,128)S(1)} fusion(s32[1536]{0:T(1024)S(1)} %compare_select_fusion.1, f32[1536,3]{1,0:T(8,128)S(1)} %copy.44, f32[]{:T(128)} %constant.14.clone.1), kind=kCustom, calls=%fused_computation.58 | custom fusion | bytes 3892 | tf_op jit(solution)/shard_map/scatter | solution.py:103
  65.0 0.1 copy.53
  65.1 0.1 convert_element_type.24
  65.2 0.1 reshape.100
  65.3 0.4 fusion.24
  65.7 0.6 copy.63
  (145 shorter events, 2.7 us)
Async XLA Ops:
  0.6 64.7 %copy-start = (bf16[2,486,486]{2,0,1:T(2,128)(2,1)S(1)}, bf16[2,486,486]{2,0,1:T(2,128)(2,1)}, u32[]{:S(2)}) copy-start(bf16[2,486,486]{2,0,1:T(2,128)(2,1)} %param.20) | copy-start | bytes 2834356
  0.6 0.9 %copy-start.5 = (s32[384]{0:T(512)S(1)}, s32[384]{0:T(512)}, u32[]{:S(2)}) copy-start(s32[384]{0:T(512)} %param.15) | copy-start | bytes 4612
  0.7 0.9 %copy-start.7 = (s32[384]{0:T(512)S(1)}, s32[384]{0:T(512)}, u32[]{:S(2)}) copy-start(s32[384]{0:T(512)} %param.16) | copy-start | bytes 4612
  1.5 0.7 %copy-start.6 = (f32[3,384]{1,0:T(4,128)S(1)}, f32[3,384]{1,0:T(4,128)}, u32[]{:S(2)}) copy-start(f32[3,384]{1,0:T(4,128)} %param.14) | copy-start | bytes 13828
  2.2 0.7 %copy-start.1 = (f32[3,384]{1,0:T(4,128)S(1)}, f32[3,384]{1,0:T(4,128)}, u32[]{:S(2)}) copy-start(f32[3,384]{1,0:T(4,128)} %param.13) | copy-start | bytes 13828
  12.7 14.5 %collective-permute-start.1 = (f32[6,768]{1,0:T(8,128)S(1)}, f32[6,768]{1,0:T(8,128)S(1)}, u32[]{:S(2)}, u32[]{:S(2)}) collective-permute-start(f32[6,768]{1,0:T(8,128)S(1)} %get-tuple-element.180), channel_id=1, source_target_pairs={{4,0},{8,4},{12,8},{16,12},{20,16},{24,20},{28,24},{5,1},{9,5},{13... | collective-permute-start | bytes 55304 | tf_op jit(solution)/shard_map/ppermute | solution.py:23
  14.0 13.2 %collective-permute-start = (f32[6,768]{1,0:T(8,128)S(1)}, f32[6,768]{1,0:T(8,128)S(1)}, u32[]{:S(2)}, u32[]{:S(2)}) collective-permute-start(f32[6,768]{1,0:T(8,128)S(1)} %get-tuple-element.179), channel_id=1, source_target_pairs={{0,4},{4,8},{8,12},{12,16},{16,20},{20,24},{24,28},{1,5},{5,9},{9,... | collective-permute-start | bytes 55304 | tf_op jit(solution)/shard_map/ppermute | solution.py:21
  25.1 0.7 %copy-start.8 = (s32[3,8]{1,0:T(4,128)S(1)}, s32[3,8]{1,0:T(4,128)}, u32[]{:S(2)}) copy-start(s32[3,8]{1,0:T(4,128)} %param.18) | copy-start | bytes 292
  25.8 0.7 copy-start.9
  27.1 0.7 copy-start.3
  27.1 0.7 copy-start.4
  50.0 10.3 %copy-start.2 = (f32[1,3,3,128]{3,1,2,0:T(4,128)}, f32[1,3,3,128]{3,1,2,0:T(4,128)S(1)}, u32[]{:S(2)}) copy-start(f32[1,3,3,128]{3,1,2,0:T(4,128)S(1)} %copy.62) | copy-start | bytes 13828
where the time goes:
time: 66.8 us; the launch traced here: 66.3 us
  blocking collectives  28.1 us (42%)
  other arithmetic  13.6 us (20%)
  local copies, waits for them, and re-layouts  13 us (19%)
  loops' own time  6.05 us (9%)
  starting transfers between devices  4.32 us (6%)
  between operations  0.83 us (1%)
    all_gather x1, blocking collectives, on_device(): lax.all_gather(blob_velocity, 'member', axis=1, tiled=True)  10.3 us
    all_gather x1, blocking collectives, on_device(): region_all = lax.all_gather(own_blobs, 'member', axis=1, tiled=True)  9.71 us
    all_gather x1, blocking collectives, on_device(): lax.all_gather(region_target, 'member', axis=0, tiled=True)  8.06 us
    reduce_sum x7, other arithmetic, stokes_sum(): return jnp.sum(direct + wall_term, axis=3)  7.13 us
    another operation x1, loops' own time, on_device(): lax.fori_loop(0, pair_rounds, one_slot, jnp.zeros(targets.shape, jnp.floa...  6.05 us
    scatter x1, local copies, waits for them, and re-layouts, on_device(): jnp.zeros((3, whole_body), jnp.float32).at[:, local_index]  4.36 us
    gather x7, local copies, waits for them, and re-layouts, one_slot(): picked = jnp.take(ext_blocks, source_ids, axis=1)  3.85 us
    unnamed x24, local copies, waits for them, and re-layouts  3.43 us
  transfers between devices with their start and end apart: 2, of which 0 were waited for; matrix products, arithmetic and copies ran while one was open for 1% of the time, Pallas kernels for 0%

commit v1 on v0

--- a/solution.py
+++ b/solution.py
@@ -73,7 +73,13 @@
     is_live = blob_platelet < plate_count
     live_mask = is_live.astype(jnp.float32)
     own_blobs = jnp.concatenate([positions, forces * live_mask[None, :]], 0)
-    region_all = lax.all_gather(own_blobs, "member", axis=1, tiled=True)
+    size = lax.axis_size("member")
+    held, parts = (own_blobs, [own_blobs])
+    for _ in range(size - 1):
+        held = lax.ppermute(held, "member", [(i_2, (i_2 + 1) % size) for i_2 in range(size)])
+        parts.insert(0, held)
+    flat = jnp.concatenate(parts, axis=1)
+    region_all = jnp.roll(flat, (lax.axis_index("member") + 1) * own_blobs.shape[1], axis=1)
     extended = padded(region_all, (("region", 1),), region_all.shape[1] // 2)
     ext_blocks = extended.reshape(6, extended.shape[1] // TILE, TILE)
     targets = positions.reshape(3, blob_count // TILE, TILE)

time: 66.8 us -> 68.8 us (1.030)
  the two profiles are of different devices: /device:TPU:0 before, /device:TPU:26 now
where the time goes in v1:
time: 68.8 us; the launch traced here: 68.3 us
  blocking collectives  16.4 us (24%)
  other arithmetic  15.4 us (22%)
  local copies, waits for them, and re-layouts  13.9 us (20%)
  starting transfers between devices  9.83 us (14%)
  loops' own time  6.82 us (10%)
  waiting for transfers between devices  4.84 us (7%)
  between operations  0.85 us (1%)
    all_gather x1, blocking collectives, on_device(): lax.all_gather(blob_velocity, 'member', axis=1, tiled=True)  9.27 us
    reduce_sum x8, other arithmetic, stokes_sum(): return jnp.sum(direct + wall_term, axis=3)  8.14 us
    all_gather x1, blocking collectives, on_device(): lax.all_gather(region_target, 'member', axis=0, tiled=True)  7.09 us
    another operation x1, loops' own time, on_device(): lax.fori_loop(0, pair_rounds, one_slot, jnp.zeros(targets.shape, jnp.floa...  6.82 us
    ppermute x3, starting transfers between devices, on_device(): lax.ppermute(held, 'member', [(i_2, (i_2 + 1) % size) for i_2 in range(si...  5.51 us
    gather x8, local copies, waits for them, and re-layouts, one_slot(): picked = jnp.take(ext_blocks, source_ids, axis=1)  4.4 us
    scatter x1, local copies, waits for them, and re-layouts, on_device(): jnp.zeros((3, whole_body), jnp.float32).at[:, local_index]  4.36 us
    unnamed x30, local copies, waits for them, and re-layouts  3.53 us
  transfers between devices with their start and end apart: 5, of which 2 were waited for; matrix products, arithmetic and copies ran while one was open for 1% of the time, Pallas kernels for 0%

profile of v1, /device:TPU:26, one launch (start us, length us, event | category | flops | bytes accessed | tf_op | source)
XLA Modules:
  0.0 68.3 jit_solution(18182112019168442217)
XLA Ops:
  0.7 0.9 %select_reduce_fusion = s32[384]{0:T(512)S(1)} fusion(s32[8]{0:T(128)} %param.17, s32[384]{0:T(512)} %param.15), kind=kLoop, calls=%fused_computation.70 | loop fusion | flops 8832 | bytes 3104 | tf_op jit(solution)/shard_map/reduce_sum | solution.py:97
  1.6 0.7 copy-done.6
  2.2 0.7 %copy-done.1 = f32[3,384]{1,0:T(4,128)S(1)} copy-done((f32[3,384]{1,0:T(4,128)S(1)}, f32[3,384]{1,0:T(4,128)}, u32[]{:S(2)}) %copy-start.1) | copy-done | bytes 4632
  2.9 1.5 %collective-permute-start = (f32[6,384]{1,0:T(8,128)S(1)}, f32[6,384]{1,0:T(8,128)S(1)}, u32[]{:S(2)}, u32[]{:S(2)}) collective-permute-start(f32[6,384]{1,0:T(8,128)S(1)} %pad_maximum_fusion), channel_id=1, source_target_pairs={{0,1},{1,2},{2,3},{3,0},{4,5},{5,6},{6,7},{7,4},{8,9},{9,10},{10,1... | collective-permute-start | bytes 27656 | tf_op jit(solution)/shard_map/ppermute | solution.py:79
  4.5 7.1 %all-gather = s32[4,1,384]{2,1,0:T(1,128)S(1)} all-gather(s32[1,1,384]{2,1,0:T(1,128)S(1)} %reshape.93), channel_id=1, replica_groups=mesh['region'=8,'member'=4] {'member'}, dimensions={0}, use_global_device_ids=true | all-gather | bytes 7680 | tf_op jit(solution)/shard_map/all_gather | solution.py:102
  11.6 1.5 %collective-permute-start.1 = (f32[6,384]{1,0:T(8,128)S(1)}, f32[6,384]{1,0:T(8,128)S(1)}, u32[]{:S(2)}, u32[]{:S(2)}) collective-permute-start(f32[6,384]{1,0:T(8,128)S(1)} %collective-permute-done), channel_id=1, source_target_pairs={{0,1},{1,2},{2,3},{3,0},{4,5},{5,6},{6,7},{7,4},{8,9},{9,10},{10,1... | collective-permute-start | bytes 27656 | tf_op jit(solution)/shard_map/ppermute | solution.py:79
  13.1 2.2 %collective-permute-done.1 = f32[6,384]{1,0:T(8,128)S(1)} collective-permute-done((f32[6,384]{1,0:T(8,128)S(1)}, f32[6,384]{1,0:T(8,128)S(1)}, u32[]{:S(2)}, u32[]{:S(2)}) %collective-permute-start.1) | collective-permute-done | bytes 9248 | tf_op jit(solution)/shard_map/ppermute | solution.py:79
  15.3 2.5 %collective-permute-start.2 = (f32[6,384]{1,0:T(8,128)S(1)}, f32[6,384]{1,0:T(8,128)S(1)}, u32[]{:S(2)}, u32[]{:S(2)}) collective-permute-start(f32[6,384]{1,0:T(8,128)S(1)} %collective-permute-done.1), channel_id=1, source_target_pairs={{0,1},{1,2},{2,3},{3,0},{4,5},{5,6},{6,7},{7,4},{8,9},{9,10},{10,1... | collective-permute-start | bytes 27656 | tf_op jit(solution)/shard_map/ppermute | solution.py:79
  17.8 0.7 copy-done.8
  18.5 0.7 copy-done.9
  19.2 0.6 reduce_max.9
  20.0 1.9 %collective-permute-start.4 = (f32[6,768]{1,0:T(8,128)S(1)}, f32[6,768]{1,0:T(8,128)S(1)}, u32[]{:S(2)}, u32[]{:S(2)}) collective-permute-start(f32[6,768]{1,0:T(8,128)S(1)} %get-tuple-element.180), channel_id=1, source_target_pairs={{4,0},{8,4},{12,8},{16,12},{20,16},{24,20},{28,24},{5,1},{9,5},{13... | collective-permute-start | bytes 55304 | tf_op jit(solution)/shard_map/ppermute | solution.py:23
  21.9 2.4 %collective-permute-start.3 = (f32[6,768]{1,0:T(8,128)S(1)}, f32[6,768]{1,0:T(8,128)S(1)}, u32[]{:S(2)}, u32[]{:S(2)}) collective-permute-start(f32[6,768]{1,0:T(8,128)S(1)} %get-tuple-element.179), channel_id=1, source_target_pairs={{0,4},{4,8},{8,12},{12,16},{16,20},{20,24},{24,28},{1,5},{5,9},{9,... | collective-permute-start | bytes 55304 | tf_op jit(solution)/shard_map/ppermute | solution.py:21
  24.4 2.6 %collective-permute-done.3 = f32[6,768]{1,0:T(8,128)S(1)} collective-permute-done((f32[6,768]{1,0:T(8,128)S(1)}, f32[6,768]{1,0:T(8,128)S(1)}, u32[]{:S(2)}, u32[]{:S(2)}) %collective-permute-start.3) | collective-permute-done | bytes 18464 | tf_op jit(solution)/shard_map/ppermute | solution.py:21
  27.1 0.6 copy-done.3
  27.8 25.3 %while.13 = (s32[]{:T(128)}, f32[3,3,128]{2,1,0:T(4,128)S(1)}, s32[]{:T(128)}, s32[3]{0:T(128)S(1)}, f32[3,384]{1,0:T(4,128)}, /*index=5*/s32[3,8]{0,1:T(8,128)S...) while((s32[]{:T(128)}, f32[3,3,128]{2,1,0:T(4,128)S(1)}, ...), condition=%wide.wide.region_8.9_spmd.clone.clone, body=%wide.wide.region_1.8_spmd.sunk.clone.clone.sunk | while | flops 6790173 | bytes 6481697 | solution.py:94
  28.5 0.6 gather_fusion
  29.2 0.3 fusion.33
  29.6 0.1 broadcast_add_fusion.3
  29.7 1.0 %fusion.34 = f32[3,3,128]{2,1,0:T(4,128)S(1)} fusion(f32[3,128,128]{2,1,0:T(8,128)S(1)} %get-tuple-element.308, f32[3,128,128]{2,1,0:T(8,128)S(1)} %get-tuple-element.311, f32[3,128,128]{2,1,0:T(8,128)S(1)} %get-tuple-element.312, f32[3,128]{1,0:T(4,128)S(1)} %get-tuple-element.313, f32[3,128,128]{2,1,0:T(8,128)S(1)} %slice_bitcast_fusion.3, ...), kind=kLoop, calls=%fused_computation.17.clone.clone.1 | loop fusion | flops 4717440 | bytes 2194956 | tf_op jit(solution)/shard_map/while/body/reduce_sum | solution.py:58
  31.5 0.6 gather_fusion
  32.3 0.3 fusion.33
  32.7 0.1 broadcast_add_fusion.3
  32.8 1.0 %fusion.34 = f32[3,3,128]{2,1,0:T(4,128)S(1)} fusion(f32[3,128,128]{2,1,0:T(8,128)S(1)} %get-tuple-element.308, f32[3,128,128]{2,1,0:T(8,128)S(1)} %get-tuple-element.311, f32[3,128,128]{2,1,0:T(8,128)S(1)} %get-tuple-element.312, f32[3,128]{1,0:T(4,128)S(1)} %get-tuple-element.313, f32[3,128,128]{2,1,0:T(8,128)S(1)} %slice_bitcast_fusion.3, ...), kind=kLoop, calls=%fused_computation.17.clone.clone.1 | loop fusion | flops 4717440 | bytes 2194956 | tf_op jit(solution)/shard_map/while/body/reduce_sum | solution.py:58
  34.6 0.6 gather_fusion
  35.4 0.3 fusion.33
  35.8 0.1 broadcast_add_fusion.3
  35.9 1.0 %fusion.34 = f32[3,3,128]{2,1,0:T(4,128)S(1)} fusion(f32[3,128,128]{2,1,0:T(8,128)S(1)} %get-tuple-element.308, f32[3,128,128]{2,1,0:T(8,128)S(1)} %get-tuple-element.311, f32[3,128,128]{2,1,0:T(8,128)S(1)} %get-tuple-element.312, f32[3,128]{1,0:T(4,128)S(1)} %get-tuple-element.313, f32[3,128,128]{2,1,0:T(8,128)S(1)} %slice_bitcast_fusion.3, ...), kind=kLoop, calls=%fused_computation.17.clone.clone.1 | loop fusion | flops 4717440 | bytes 2194956 | tf_op jit(solution)/shard_map/while/body/reduce_sum | solution.py:58
  37.7 0.6 gather_fusion
  38.4 0.3 fusion.33
  39.0 1.0 %fusion.34 = f32[3,3,128]{2,1,0:T(4,128)S(1)} fusion(f32[3,128,128]{2,1,0:T(8,128)S(1)} %get-tuple-element.308, f32[3,128,128]{2,1,0:T(8,128)S(1)} %get-tuple-element.311, f32[3,128,128]{2,1,0:T(8,128)S(1)} %get-tuple-element.312, f32[3,128]{1,0:T(4,128)S(1)} %get-tuple-element.313, f32[3,128,128]{2,1,0:T(8,128)S(1)} %slice_bitcast_fusion.3, ...), kind=kLoop, calls=%fused_computation.17.clone.clone.1 | loop fusion | flops 4717440 | bytes 2194956 | tf_op jit(solution)/shard_map/while/body/reduce_sum | solution.py:58
  40.8 0.6 gather_fusion
  41.5 0.3 fusion.33
  42.1 1.0 %fusion.34 = f32[3,3,128]{2,1,0:T(4,128)S(1)} fusion(f32[3,128,128]{2,1,0:T(8,128)S(1)} %get-tuple-element.308, f32[3,128,128]{2,1,0:T(8,128)S(1)} %get-tuple-element.311, f32[3,128,128]{2,1,0:T(8,128)S(1)} %get-tuple-element.312, f32[3,128]{1,0:T(4,128)S(1)} %get-tuple-element.313, f32[3,128,128]{2,1,0:T(8,128)S(1)} %slice_bitcast_fusion.3, ...), kind=kLoop, calls=%fused_computation.17.clone.clone.1 | loop fusion | flops 4717440 | bytes 2194956 | tf_op jit(solution)/shard_map/while/body/reduce_sum | solution.py:58
  43.9 0.6 gather_fusion
  44.6 0.3 fusion.33
  45.1 1.0 %fusion.34 = f32[3,3,128]{2,1,0:T(4,128)S(1)} fusion(f32[3,128,128]{2,1,0:T(8,128)S(1)} %get-tuple-element.308, f32[3,128,128]{2,1,0:T(8,128)S(1)} %get-tuple-element.311, f32[3,128,128]{2,1,0:T(8,128)S(1)} %get-tuple-element.312, f32[3,128]{1,0:T(4,128)S(1)} %get-tuple-element.313, f32[3,128,128]{2,1,0:T(8,128)S(1)} %slice_bitcast_fusion.3, ...), kind=kLoop, calls=%fused_computation.17.clone.clone.1 | loop fusion | flops 4717440 | bytes 2194956 | tf_op jit(solution)/shard_map/while/body/reduce_sum | solution.py:58
  46.9 0.6 gather_fusion
  47.7 0.3 fusion.33
  48.2 1.0 %fusion.34 = f32[3,3,128]{2,1,0:T(4,128)S(1)} fusion(f32[3,128,128]{2,1,0:T(8,128)S(1)} %get-tuple-element.308, f32[3,128,128]{2,1,0:T(8,128)S(1)} %get-tuple-element.311, f32[3,128,128]{2,1,0:T(8,128)S(1)} %get-tuple-element.312, f32[3,128]{1,0:T(4,128)S(1)} %get-tuple-element.313, f32[3,128,128]{2,1,0:T(8,128)S(1)} %slice_bitcast_fusion.3, ...), kind=kLoop, calls=%fused_computation.17.clone.clone.1 | loop fusion | flops 4717440 | bytes 2194956 | tf_op jit(solution)/shard_map/while/body/reduce_sum | solution.py:58
  50.0 0.6 gather_fusion
  50.8 0.3 fusion.33
  51.3 1.0 %fusion.34 = f32[3,3,128]{2,1,0:T(4,128)S(1)} fusion(f32[3,128,128]{2,1,0:T(8,128)S(1)} %get-tuple-element.308, f32[3,128,128]{2,1,0:T(8,128)S(1)} %get-tuple-element.311, f32[3,128,128]{2,1,0:T(8,128)S(1)} %get-tuple-element.312, f32[3,128]{1,0:T(4,128)S(1)} %get-tuple-element.313, f32[3,128,128]{2,1,0:T(8,128)S(1)} %slice_bitcast_fusion.3, ...), kind=kLoop, calls=%fused_computation.17.clone.clone.1 | loop fusion | flops 4717440 | bytes 2194956 | tf_op jit(solution)/shard_map/while/body/reduce_sum | solution.py:58
  53.1 9.3 %all_gather.7 = f32[3,1536]{1,0:T(4,128)S(1)} all-gather(f32[3,384]{1,0:T(4,128)S(1)} %bitcast.48), channel_id=1, replica_groups=mesh['region'=8,'member'=4] {'member'}, dimensions={1}, use_global_device_ids=true | all-gather | bytes 23040 | tf_op jit(solution)/shard_map/all_gather | solution.py:101
  62.4 0.3 copy.44
  62.7 4.4 %scatter_custom_fusion = f32[3,324]{0,1:T(8,128)S(1)} fusion(s32[1536]{0:T(1024)S(1)} %compare_select_fusion.1, f32[1536,3]{1,0:T(8,128)S(1)} %copy.44, f32[]{:T(128)} %constant.42.clone.1), kind=kCustom, calls=%fused_computation.58 | custom fusion | bytes 3892 | tf_op jit(solution)/shard_map/scatter | solution.py:109
  67.4 0.4 fusion.24
  67.7 0.6 copy.63
  (179 shorter events, 4.0 us)
Async XLA Ops:
  0.6 66.7 %copy-start = (bf16[2,486,486]{2,0,1:T(2,128)(2,1)S(1)}, bf16[2,486,486]{2,0,1:T(2,128)(2,1)}, u32[]{:S(2)}) copy-start(bf16[2,486,486]{2,0,1:T(2,128)(2,1)} %param.20) | copy-start | bytes 2834356
  0.6 0.9 %copy-start.5 = (s32[384]{0:T(512)S(1)}, s32[384]{0:T(512)}, u32[]{:S(2)}) copy-start(s32[384]{0:T(512)} %param.15) | copy-start | bytes 4612
  0.7 0.9 %copy-start.7 = (s32[384]{0:T(512)S(1)}, s32[384]{0:T(512)}, u32[]{:S(2)}) copy-start(s32[384]{0:T(512)} %param.16) | copy-start | bytes 4612
  1.5 0.7 %copy-start.6 = (f32[3,384]{1,0:T(4,128)S(1)}, f32[3,384]{1,0:T(4,128)}, u32[]{:S(2)}) copy-start(f32[3,384]{1,0:T(4,128)} %param.14) | copy-start | bytes 13828
  2.2 0.7 %copy-start.1 = (f32[3,384]{1,0:T(4,128)S(1)}, f32[3,384]{1,0:T(4,128)}, u32[]{:S(2)}) copy-start(f32[3,384]{1,0:T(4,128)} %param.13) | copy-start | bytes 13828
  2.9 8.6 %collective-permute-start = (f32[6,384]{1,0:T(8,128)S(1)}, f32[6,384]{1,0:T(8,128)S(1)}, u32[]{:S(2)}, u32[]{:S(2)}) collective-permute-start(f32[6,384]{1,0:T(8,128)S(1)} %pad_maximum_fusion), channel_id=1, source_target_pairs={{0,1},{1,2},{2,3},{3,0},{4,5},{5,6},{6,7},{7,4},{8,9},{9,10},{10,1... | collective-permute-start | bytes 27656 | tf_op jit(solution)/shard_map/ppermute | solution.py:79
  11.6 3.7 %collective-permute-start.1 = (f32[6,384]{1,0:T(8,128)S(1)}, f32[6,384]{1,0:T(8,128)S(1)}, u32[]{:S(2)}, u32[]{:S(2)}) collective-permute-start(f32[6,384]{1,0:T(8,128)S(1)} %collective-permute-done), channel_id=1, source_target_pairs={{0,1},{1,2},{2,3},{3,0},{4,5},{5,6},{6,7},{7,4},{8,9},{9,10},{10,1... | collective-permute-start | bytes 27656 | tf_op jit(solution)/shard_map/ppermute | solution.py:79
  15.3 4.5 %collective-permute-start.2 = (f32[6,384]{1,0:T(8,128)S(1)}, f32[6,384]{1,0:T(8,128)S(1)}, u32[]{:S(2)}, u32[]{:S(2)}) collective-permute-start(f32[6,384]{1,0:T(8,128)S(1)} %collective-permute-done.1), channel_id=1, source_target_pairs={{0,1},{1,2},{2,3},{3,0},{4,5},{5,6},{6,7},{7,4},{8,9},{9,10},{10,1... | collective-permute-start | bytes 27656 | tf_op jit(solution)/shard_map/ppermute | solution.py:79
  17.8 0.7 copy-start.8
  18.5 0.7 copy-start.9
  20.0 4.4 %collective-permute-start.4 = (f32[6,768]{1,0:T(8,128)S(1)}, f32[6,768]{1,0:T(8,128)S(1)}, u32[]{:S(2)}, u32[]{:S(2)}) collective-permute-start(f32[6,768]{1,0:T(8,128)S(1)} %get-tuple-element.180), channel_id=1, source_target_pairs={{4,0},{8,4},{12,8},{16,12},{20,16},{24,20},{28,24},{5,1},{9,5},{13... | collective-permute-start | bytes 55304 | tf_op jit(solution)/shard_map/ppermute | solution.py:23
  21.9 5.1 %collective-permute-start.3 = (f32[6,768]{1,0:T(8,128)S(1)}, f32[6,768]{1,0:T(8,128)S(1)}, u32[]{:S(2)}, u32[]{:S(2)}) collective-permute-start(f32[6,768]{1,0:T(8,128)S(1)} %get-tuple-element.179), channel_id=1, source_target_pairs={{0,4},{4,8},{8,12},{12,16},{16,20},{20,24},{24,28},{1,5},{5,9},{9,... | collective-permute-start | bytes 55304 | tf_op jit(solution)/shard_map/ppermute | solution.py:21
  27.1 0.7 copy-start.3
  27.1 0.7 copy-start.4
  53.1 9.3 %copy-start.2 = (f32[1,3,3,128]{3,1,2,0:T(4,128)}, f32[1,3,3,128]{3,1,2,0:T(4,128)S(1)}, u32[]{:S(2)}) copy-start(f32[1,3,3,128]{3,1,2,0:T(4,128)S(1)} %copy.62) | copy-start | bytes 13828
